TPU v7x, 256 devices: a whole 4x4x8 slice. The times are simulated.
256 devices in a mesh: gx: 16 (over y_lo, z), gy: 16 (over x, y_hi, core).
Axes of the slice: x: 4, y: 4 (y_hi: 2, y_lo: 2; y = y_hi * 2 + y_lo), z: 8, core: 2. Of those that a mesh axis runs over, the one named last changes fastest.
Arguments:
- tokens: bfloat16 [4, 128, 128, 256], P(None, 'gx', 'gy'), may hold values from -6 to 6
- syndrome: int32 [4, 128, 128], P(None, 'gx', 'gy'), may hold values 0 or 1
- check_plan_step: int32 [4, 128, 128], P(None, 'gx', 'gy'), may hold values from 0 to 7
- offsets: int32 [6, 2], replicated, may hold values from 0 to 8, as said below
- flip_vector: float32 [256], replicated, may hold values from -3 to 3
- plan_step_embedding: float32 [8, 256], replicated, may hold values from -3 to 3
- gain_tanner: float32 [256], replicated, may hold values from 0.5 to 1.5
- w_query: bfloat16 [256, 256], replicated, may hold values from -0.375 to 0.375
- w_key_value: bfloat16 [256, 512], replicated, may hold values from -0.375 to 0.375
- w_merge: bfloat16 [256, 256], replicated, may hold values from -0.375 to 0.375
- gain_time: float32 [256], replicated, may hold values from 0.5 to 1.5
- w_temporal: bfloat16 [256, 768], replicated, may hold values from -0.375 to 0.375
- w_temporal_out: bfloat16 [256, 256], replicated, may hold values from -0.375 to 0.375
- gain_ffn: float32 [256], replicated, may hold values from 0.5 to 1.5
- w_ffn_up: bfloat16 [256, 1024], replicated, may hold values from -0.375 to 0.375
- w_ffn_down: bfloat16 [1024, 256], replicated, may hold values from -0.1875 to 0.1875
- cotangent: bfloat16 [4, 128, 128, 256], P(None, 'gx', 'gy'), may hold values from -6 to 6
Outputs:
- token_grad: bfloat16 [4, 128, 128, 256], P(None, 'gx', 'gy')
- grad_flip: float32 [256], replicated
- plan_step_gradient: float32 [8, 256], replicated
- grad_gain_tanner: float32 [256], replicated
- grad_query: float32 [256, 256], replicated
- grad_key_value: float32 [256, 512], replicated
- grad_merge: float32 [256, 256], replicated
- grad_gain_time: float32 [256], replicated
- grad_temporal: float32 [256, 768], replicated
- grad_temporal_out: float32 [256, 256], replicated
- grad_gain_ffn: float32 [256], replicated
- grad_up: float32 [256, 1024], replicated
- grad_down: float32 [1024, 256], replicated
Inputs may be any that keep to these rules, and one draw needn't show every extreme that they name: `offsets`: rows 0, 4 and 5 are (e, 0) and rows 1, 2 and 3 are (0, e), with e from 1 to 8; rows 0 and 3 have e = 8.
All inputs are finite; a program needn't handle non-finite values. No bound on the sum of `syndrome` on one device may be relied on, other than what follows from the above.
Results may differ from a plain program's by a relative error of at most 0.022.
Values may be sent and summed in bfloat16 or wider, within the bound.
A program may use at most 64 MiB of HBM per device.

v0:
```python
import math

import jax
import jax.numpy as jnp
from jax import lax
from jax.experimental import pallas as pl
from jax.experimental.pallas import tpu as pltpu
from jax.sharding import PartitionSpec as P

WIDTH = 256
HEADDIM = 32
FF = 1024
PLAN_STEP_COUNT = 8
TOKENS = 256
NEIGHBOURS = 7
ROUNDS = 4
EPS = 1e-05
CAP = 4.0
ROOT = math.sqrt(HEADDIM)
GELU = math.sqrt(2 / math.pi)

MESH = pl.DeviceIdType.MESH
HALF = 1024
RESULT_ROWS = 8 * HALF
PLANE_STEPS = sorted(
    [(x, y) for x in range(4) for y in range(4) if x or y], key=lambda at: -(at[0] % 2 + at[1] % 2 + 2 * (at[0] == 2) + 2 * (at[1] == 2)))
Z_STEPS = (4, 3, 5, 2, 6, 1, 7)
SMALL_ROWS = 16


class Place:
    def __init__(self):
        self.gx = lax.axis_index("gx")
        self.gy = lax.axis_index("gy")
        self.z = lax.rem(self.gx, 8)
        self.y_lo = lax.div(self.gx, 8)
        self.core = lax.rem(self.gy, 2)
        self.y_hi = lax.rem(lax.div(self.gy, 2), 2)
        self.x = lax.div(self.gy, 4)
        self.y = self.y_hi * 2 + self.y_lo

    def other_core(self):
        return (self.gx, self.gy + 1 - 2 * self.core)

    def at_x(self, x):
        return (self.gx, x * 4 + self.y_hi * 2 + self.core)

    def at_y(self, y):
        return (lax.rem(y, 2) * 8 + self.z, self.x * 4 + lax.div(y, 2) * 2 + self.core)

    def in_plane(self, x, y):
        return (lax.rem(y, 2) * 8 + self.z, x * 4 + lax.div(y, 2) * 2 + self.core)

    def at_z(self, z):
        return (self.y_lo * 8 + z, self.gy)

    def greeted(self):
        peers = [self.row_tile(1), self.column_tile(1), self.row_tile(15), self.column_tile(15)]
        peers.append(self.other_core())
        for step_x, step_y in PLANE_STEPS:
            peers.append(self.in_plane(lax.rem(self.x + step_x, 4), lax.rem(self.y + step_y, 4)))
        for step in range(1, 8):
            peers.append(self.at_z(lax.rem(self.z + step, 8)))
        return peers

    def row_tile(self, step):
        return (lax.rem(self.gx + step, 16), self.gy)

    def column_tile(self, step):
        return (self.gx, lax.rem(self.gy + step, 16))


def greet(peers):
    barrier = pltpu.get_barrier_semaphore()
    for peer in peers:
        pl.semaphore_signal(barrier, inc=1, device_id=peer, device_id_type=MESH)
    return barrier, len(peers)


def rows(start, count):
    return pl.ds(pl.multiple_of(start, min(count, 16)), count)


class Sum:
    @staticmethod
    def scratch(half):
        bf16 = jnp.bfloat16
        return (
            pltpu.VMEM((half, 128), bf16),
            pltpu.VMEM((half, 128), bf16),
            pltpu.VMEM((15, half // 16, 128), bf16),
            pltpu.VMEM((8, half // 16, 128), bf16),
            pltpu.SemaphoreType.DMA((54,)),
            pltpu.SemaphoreType.DMA((54,)),
        )

    def __init__(self, place, half, base, source, result, scratch):
        self.place = place
        self.half = half
        self.chunk = half // 16
        self.base = base + place.core * half
        self.source = source
        self.result = result
        self.from_core, self.one, self.in_two, self.along_z, self.send, self.recv = scratch

    def copy(self, slot, source, target, peer):
        copy = pltpu.make_async_remote_copy(
            src_ref=source,
            dst_ref=target,
            send_sem=self.send.at[slot],
            recv_sem=self.recv.at[slot],
            device_id=peer,
            device_id_type=MESH,
        )
        copy.start()
        return copy

    def to_plane(self, slot, source, target):
        p = self.place
        self.copies = []
        for index, (step_x, step_y) in enumerate(PLANE_STEPS):
            x, y = lax.rem(p.x + step_x, 4), lax.rem(p.y + step_y, 4)
            self.copies.append(
                self.copy(slot + index, source((x * 4 + y) * self.chunk), target(index), p.in_plane(x, y)))

    def in_result(self, x, y):
        return self.result.at[rows(self.base + (x * 4 + y) * self.chunk, self.chunk)]

    def core_out(self):
        other = rows((1 - self.place.core) * self.half, self.half)
        self.core_copy = self.copy(0, self.source.at[other], self.from_core, self.place.other_core())

    def core_in(self):
        self.core_copy.wait()
        own = self.source[rows(self.place.core * self.half, self.half)]
        self.one[...] = (own.astype(jnp.float32) + self.from_core[...].astype(jnp.float32)).astype(jnp.bfloat16)
        self.to_plane(
            1, lambda at: self.one.at[rows(at, self.chunk)], lambda index: self.in_two.at[index])

    def plane_in(self):
        p = self.place
        for copy in self.copies:
            copy.wait()
        total = self.one[rows((p.x * 4 + p.y) * self.chunk, self.chunk)].astype(jnp.float32)
        for index in range(15):
            total = total + self.in_two[index].astype(jnp.float32)
        self.along_z[p.z] = total.astype(jnp.bfloat16)
        own = self.along_z.at[p.z]
        self.copies = []
        for index, step in enumerate(Z_STEPS):
            self.copies.append(self.copy(16 + index, own, own, p.at_z(lax.rem(p.z + step, 8))))

    def z_in(self):
        p = self.place
        for copy in self.copies:
            copy.wait()
        total = self.along_z[0].astype(jnp.float32)
        for index in range(1, 8):
            total = total + self.along_z[index].astype(jnp.float32)
        self.result[rows(self.base + (p.x * 4 + p.y) * self.chunk, self.chunk)] = total.astype(jnp.bfloat16)
        own = self.in_result(p.x, p.y)
        self.to_plane(23, lambda at: own, lambda index: own)
        self.core_copies = [self.copy(38, own, own, p.other_core())]

    def plane_gathered(self):
        p = self.place
        for index in reversed(range(15)):
            self.copies[index].wait()
            step_x, step_y = PLANE_STEPS[index]
            chunk = self.in_result(lax.rem(p.x + 4 - step_x, 4), lax.rem(p.y + 4 - step_y, 4))
            self.core_copies.append(self.copy(39 + index, chunk, chunk, p.other_core()))

    def finish(self):
        for copy in self.core_copies:
            copy.wait()


class TwoStepSum(Sum):
    @staticmethod
    def scratch(half):
        bf16 = jnp.bfloat16
        return (
            pltpu.VMEM((half, 128), bf16),
            pltpu.VMEM((half, 128), bf16),
            pltpu.VMEM((6, half // 8, 128), bf16),
            pltpu.VMEM((2, half // 8, 128), bf16),
            pltpu.VMEM((6, half // 32, 128), bf16),
            pltpu.VMEM((8, half // 16, 128), bf16),
            pltpu.SemaphoreType.DMA((40,)),
            pltpu.SemaphoreType.DMA((40,)),
        )

    def __init__(self, place, half, base, source, result, scratch):
        self.place = place
        self.half = half
        self.strip = half // 8
        self.chunk = half // 32
        self.base = base + place.core * half
        self.source = source
        self.result = result
        (self.from_core, self.one, self.in_one, self.two, self.in_two, self.along_z, self.send, self.recv) = scratch

    def both_ways(self, slot, first_along_x, first, second, first_target, second_target):
        p = self.place
        self.copies = []
        for index, step in enumerate((2, 1, 3)):
            x, y = lax.rem(p.x + step, 4), lax.rem(p.y + step, 4)
            of_first, of_second = ((x, p.at_x(x)), (y, p.at_y(y)))[:: 1 if first_along_x else -1]
            self.copies.append(
                self.copy(slot + index, first(of_first[0]), first_target(index), of_first[1]))
            self.copies.append(
                self.copy(slot + 3 + index, second(of_second[0]), second_target(index), of_second[1]))

    def core_in(self):
        self.core_copy.wait()
        own = self.source[rows(self.place.core * self.half, self.half)]
        self.one[...] = (own.astype(jnp.float32) + self.from_core[...].astype(jnp.float32)).astype(jnp.bfloat16)
        middle = self.half // 2
        self.both_ways(
            1,
            True,
            lambda x: self.one.at[rows(x * self.strip, self.strip)],
            lambda y: self.one.at[rows(middle + y * self.strip, self.strip)],
            lambda index: self.in_one.at[index],
            lambda index: self.in_one.at[3 + index],
        )

    def strip_in(self):
        p = self.place
        for copy in self.copies:
            copy.wait()
        for part, own in ((0, p.x * self.strip), (1, self.half // 2 + p.y * self.strip)):
            total = self.one[rows(own, self.strip)].astype(jnp.float32)
            for index in range(3):
                total = total + self.in_one[part * 3 + index].astype(jnp.float32)
            self.two[part] = total.astype(jnp.bfloat16)
        self.both_ways(
            7,
            False,
            lambda y: self.two.at[0, rows(y * self.chunk, self.chunk)],
            lambda x: self.two.at[1, rows(x * self.chunk, self.chunk)],
            lambda index: self.in_two.at[index],
            lambda index: self.in_two.at[3 + index],
        )

    def plane_in(self):
        p = self.place
        for copy in self.copies:
            copy.wait()
        for part, own in ((0, p.y * self.chunk), (1, p.x * self.chunk)):
            total = self.two[part, rows(own, self.chunk)].astype(jnp.float32)
            for index in range(3):
                total = total + self.in_two[part * 3 + index].astype(jnp.float32)
            self.along_z[p.z, part * self.chunk : (part + 1) * self.chunk] = total.astype(jnp.bfloat16)
        own = self.along_z.at[p.z]
        self.copies = []
        for index, step in enumerate(Z_STEPS):
            self.copies.append(self.copy(13 + index, own, own, p.at_z(lax.rem(p.z + step, 8))))

    def z_in(self):
        p = self.place
        for copy in self.copies:
            copy.wait()
        total = self.along_z[0].astype(jnp.float32)
        for index in range(1, 8):
            total = total + self.along_z[index].astype(jnp.float32)
        total = total.astype(jnp.bfloat16)
        first = rows(self.base + p.x * self.strip + p.y * self.chunk, self.chunk)
        second = rows(self.base + self.half // 2 + p.y * self.strip + p.x * self.chunk, self.chunk)
        self.result[first] = total[: self.chunk]
        self.result[second] = total[self.chunk :]
        first, second = self.result.at[first], self.result.at[second]
        self.both_ways(
            20, False, lambda _: first, lambda _: second, lambda _: first, lambda _: second)

    def strip_of(self, part, index):
        return self.result.at[rows(self.base + part * (self.half // 2) + index * self.strip, self.strip)]

    def strip_gathered(self):
        p = self.place
        for copy in self.copies:
            copy.wait()
        first, second = self.strip_of(0, p.x), self.strip_of(1, p.y)
        self.both_ways(
            26, True, lambda _: first, lambda _: second, lambda _: first, lambda _: second)
        self.core_copies = [
            self.copy(32, first, first, p.other_core()), self.copy(33, second, second, p.other_core())]

    def plane_gathered(self):
        p = self.place
        for index in reversed(range(6)):
            self.copies[index].wait()
            part, step = index % 2, (2, 1, 3)[index // 2]
            strip = self.strip_of(part, lax.rem((p.x, p.y)[part] + 4 - step, 4))
            self.core_copies.append(self.copy(34 + index, strip, strip, p.other_core()))


class SmallSum:
    SCRATCH = (
        pltpu.VMEM((2, SMALL_ROWS, 256), jnp.bfloat16),
        pltpu.VMEM((16, SMALL_ROWS, 256), jnp.bfloat16),
        pltpu.VMEM((8, SMALL_ROWS, 256), jnp.bfloat16),
        pltpu.SemaphoreType.DMA((23,)),
        pltpu.SemaphoreType.DMA((23,)),
    )

    def __init__(self, place, scratch):
        self.place = place
        self.slots = scratch[:3]
        self.send, self.recv = scratch[3:]

    def out(self, stage, value):
        p = self.place
        self.stage = stage
        slots = self.slots[stage]
        mine = (p.core, p.x * 4 + p.y, p.z)[stage]
        if stage == 0:
            peers = [p.other_core()]
        elif stage == 1:
            peers = [p.in_plane(lax.rem(p.x + x, 4), lax.rem(p.y + y, 4)) for x, y in PLANE_STEPS]
        else:
            peers = [p.at_z(lax.rem(p.z + step, 8)) for step in Z_STEPS]
        slots[mine] = value.astype(jnp.bfloat16)
        self.copies = []
        for index, peer in enumerate(peers):
            copy = pltpu.make_async_remote_copy(
                src_ref=slots.at[mine],
                dst_ref=slots.at[mine],
                send_sem=self.send.at[(0, 1, 16)[stage] + index],
                recv_sem=self.recv.at[(0, 1, 16)[stage] + index],
                device_id=peer,
                device_id_type=MESH,
            )
            copy.start()
            self.copies.append(copy)

    def total(self):
        for copy in self.copies:
            copy.wait()
        slots = self.slots[self.stage]
        total = slots[0].astype(jnp.float32)
        for index in range(1, slots.shape[0]):
            total = total + slots[index].astype(jnp.float32)
        return total


def dot(left, right):
    return lax.dot_general(left, right, (((1,), (0,)), ((), ())), preferred_element_type=jnp.float32)


def dot_back(grad, weight):
    return lax.dot_general(grad, weight, (((1,), (1,)), ((), ())), preferred_element_type=jnp.float32)


def dot_weight(inputs, grad):
    return lax.dot_general(inputs, grad, (((0,), (0,)), ((), ())), preferred_element_type=jnp.float32)


def low(value):
    return value.astype(jnp.bfloat16)


def wide(value):
    return value.astype(jnp.float32)


def halves(value):
    upper = low(value)
    return upper, low(value - wide(upper))


def ones(mask):
    return low(jnp.where(mask, 1.0, 0.0))


def iota(shape, axis):
    return lax.broadcasted_iota(jnp.int32, shape, axis)


def norm(stream, gain):
    inverse = lax.rsqrt(jnp.mean(stream * stream, axis=-1, keepdims=True) + EPS)
    unit = stream * inverse
    return unit, inverse, low(unit * gain)


def norm_back(grad, unit, inverse, gain):
    scaled = grad * gain
    along = jnp.mean(scaled * unit, axis=-1, keepdims=True)
    return inverse * (scaled - unit * along), jnp.sum(grad * unit, axis=0, keepdims=True)


def over_neighbours(value):
    value = value + pltpu.roll(value, 64, 1)
    value = value + pltpu.roll(value, 32, 1)
    return value + pltpu.roll(value, 16, 1)


class Attention:
    def __init__(self, gather_ref, spread_ref, order, key, value, allowed):
        self.gather_ref = gather_ref
        self.spread_ref = spread_ref
        self.count = len(order)
        self.order = order
        self.key = key
        self.value = value
        self.allowed = allowed

    def gather(self, products):
        total = jnp.zeros((TOKENS, 128), jnp.float32)
        for index in range(self.count):
            matrix = self.gather_ref[index * WIDTH : (index + 1) * WIDTH]
            upper, lower = halves(products(index))
            total = total + dot(upper, matrix) + dot(lower, matrix)
        return total

    def spread(self, small, index):
        both = jnp.concatenate(halves(small), axis=1)
        return dot(both, self.spread_ref[:, index * WIDTH : (index + 1) * WIDTH])

    def forward(self, query):
        score = self.gather(lambda index: query * self.key(index))
        self.capped = jnp.tanh(score * (1.0 / (ROOT * CAP)))
        weight = jnp.where(self.allowed, jnp.exp(CAP * self.capped), 0.0)
        self.share = weight / over_neighbours(weight)
        mixed = jnp.zeros((TOKENS, WIDTH), jnp.float32)
        for index in range(self.count):
            mixed = mixed + self.spread(self.share, index) * self.value(index)
        return mixed

    def backward(self, query, grad, put):
        grad_share = self.gather(lambda index: grad * self.value(index))
        along = over_neighbours(self.share * grad_share)
        grad_score = self.share * (grad_share - along) * (1.0 - self.capped * self.capped) * (1.0 / ROOT)
        grad_query = jnp.zeros((TOKENS, WIDTH), jnp.float32)
        for index in self.order:
            spread = self.spread(grad_score, index)
            grad_query = grad_query + spread * self.key(index)
            put(index, spread * query, self.spread(self.share, index) * grad)
        return grad_query


def turn(value, by):
    return pltpu.roll(value.reshape(TOKENS // 8, 8, -1), by, 1).reshape(TOKENS, -1)


def window_kernel(
    tokens_ref,
    syndrome_ref,
    step_ref,
    offsets_ref,
    flip_ref,
    embedding_ref,
    gain_tanner_ref,
    w_query_hbm,
    w_key_value_hbm,
    w_merge_hbm,
    gain_time_ref,
    w_temporal_hbm,
    w_temporal_out_hbm,
    gain_ffn_ref,
    w_up_hbm,
    w_down_hbm,
    cotangent_hbm,
    result_ref,
    small_result_ref,
    token_grad_ref,
    w_query_ref,
    w_key_value_ref,
    w_merge_ref,
    w_temporal_ref,
    w_temporal_out_ref,
    w_up_ref,
    w_down_ref,
    cotangent_ref,
    loaded,
    early_ref,
    middle_ref,
    late_ref,
    gather_ref,
    spread_ref,
    hidden_ref,
    back_out_ref,
    back_in_ref,
    ahead_ref,
    near_ref,
    padded_ref,
    own_grad_ref,
    rows_grad_ref,
    columns_grad_ref,
    activated_ref,
    before_ref,
    packed_ref,
    grad_packed_ref,
    halo_send,
    halo_recv,
    *scratch,
):
    place = Place()
    barrier, greeted = greet(place.greeted())
    loads = []
    for index, (source, target) in enumerate((
        (w_query_hbm, w_query_ref),
        (w_key_value_hbm, w_key_value_ref),
        (w_merge_hbm, w_merge_ref),
        (w_temporal_hbm, w_temporal_ref),
        (w_temporal_out_hbm, w_temporal_out_ref),
        (w_up_hbm, w_up_ref),
        (w_down_hbm, w_down_ref),
        (cotangent_hbm, cotangent_ref),
    )):
        load = pltpu.make_async_copy(source, target, loaded.at[index])
        load.start()
        loads.append(load)
    groups = ((TwoStepSum, 2 * HALF, 0, early_ref), (TwoStepSum, HALF, 4 * HALF, middle_ref), (TwoStepSum, HALF, 6 * HALF, late_ref))
    ends = [len(SmallSum.SCRATCH)]
    for kind, half, _, _ in groups:
        ends.append(ends[-1] + len(kind.scratch(half)))
    early, middle, late = (
        kind(place, half, base, source, result_ref, scratch[ends[index] : ends[index + 1]])
        for index, (kind, half, base, source) in enumerate(groups))
    small = SmallSum(place, scratch[: ends[0]])

    def send(slot, source, target, peer):
        copy = pltpu.make_async_remote_copy(
            src_ref=source,
            dst_ref=target,
            send_sem=halo_send.at[slot],
            recv_sem=halo_recv.at[slot],
            device_id=peer,
            device_id_type=MESH,
        )
        copy.start()
        return copy

    code = low(wide(step_ref[...] + 16 * syndrome_ref[...]))
    site_row = ones(lax.div(iota((TOKENS, 32), 0), 8) == iota((TOKENS, 32), 1))
    site_column = lax.rem(iota((TOKENS, 8), 0), 8) == iota((TOKENS, 8), 1)
    code = jnp.sum(jnp.where(site_column, dot(site_row, code), 0.0), axis=1, keepdims=True)
    lane = iota((TOKENS, 16), 1)
    lane_value = wide(lane)
    flipped = jnp.where(code > 15.5, 1.0, 0.0)
    on_step = jnp.where(code - 16.0 * flipped == lane_value, 1.0, 0.0)
    features = low(jnp.where(lane < 8, on_step, jnp.where(lane == 8, flipped, 0.0)))
    table = jnp.concatenate(
        [embedding_ref[...], jnp.broadcast_to(flip_ref[...], (8, WIDTH))], axis=0)
    upper = low(table)
    next_upper, lower = halves(table - wide(upper))
    embedded = wide(tokens_ref[...]) + (dot(features, upper) + (dot(features, next_upper) + dot(features, lower)))
    unit_one, inverse_one, hidden_one = norm(embedded, gain_tanner_ref[...])
    hidden_ref[:TOKENS] = hidden_one
    pl.semaphore_wait(barrier, greeted)
    own_hidden = hidden_ref.at[pl.ds(0, TOKENS)]
    ahead_rows = send(0, own_hidden, hidden_ref.at[pl.ds(TOKENS, TOKENS)], place.row_tile(15))
    ahead_columns = send(1, own_hidden, hidden_ref.at[pl.ds(2 * TOKENS, TOKENS)], place.column_tile(15))

    for index in range(2):
        padded_ref[index, :, 0:8] = jnp.zeros((ROUNDS, 8, 8, 2 * WIDTH), jnp.float32)
        padded_ref[index, :, 16:24] = jnp.zeros((ROUNDS, 8, 8, 2 * WIDTH), jnp.float32)

    shape = (NEIGHBOURS * WIDTH, 128)
    feature = iota(shape, 0)
    gather_ref[...] = ones(
        lax.div(feature, WIDTH) * 16 + lax.div(lax.rem(feature, WIDTH), HEADDIM) == iota(shape, 1))
    shape = (256, NEIGHBOURS * WIDTH)
    feature = iota(shape, 1)
    spread_ref[...] = ones(
        lax.div(feature, WIDTH) * 16 + lax.div(lax.rem(feature, WIDTH), HEADDIM) == lax.rem(iota(shape, 0), 128))

    for load in loads[:3]:
        load.wait()
    query = wide(low(dot(hidden_one, w_query_ref[...])))
    own = wide(low(dot(hidden_one, w_key_value_ref[...])))
    near_ref[0] = own
    ahead_ref[:, 0:8] = own.reshape(ROUNDS, 8, 8, 2 * WIDTH)
    ahead_rows.wait()
    rows_ahead = wide(low(dot(hidden_ref[TOKENS : 2 * TOKENS], w_key_value_ref[...])))
    near_ref[1] = rows_ahead
    ahead_ref[:, 8:16] = rows_ahead.reshape(ROUNDS, 8, 8, 2 * WIDTH)
    for index in (5, 6):
        near_ref[index] = ahead_ref[:, pl.ds(offsets_ref[0, index - 1], 8)].reshape(TOKENS, 2 * WIDTH)
    ahead_columns.wait()
    columns_ahead = wide(low(dot(hidden_ref[2 * TOKENS :], w_key_value_ref[...])))
    near_ref[4] = columns_ahead
    column = lax.rem(iota((TOKENS, 1), 0), 8)
    for index in (2, 3):
        by = offsets_ref[1, index - 1]
        near_ref[index] = jnp.where(column < 8 - by, turn(own, 8 - by), turn(columns_ahead, 8 - by))
    lanes = iota((TOKENS, 128), 1)
    tanner = Attention(
        gather_ref,
        spread_ref,
        (0, 1, 4, 2, 3, 5, 6),
        lambda index: near_ref[index, :, :WIDTH],
        lambda index: near_ref[index, :, WIDTH:],
        lanes < NEIGHBOURS * 16,
    )
    mixed_one = low(tanner.forward(query))
    after_tanner = embedded + dot(mixed_one, w_merge_ref[...])

    for load in loads[3:]:
        load.wait()
    unit_two, inverse_two, hidden_two = norm(after_tanner, gain_time_ref[...])
    packed_ref[...] = wide(low(dot(hidden_two, w_temporal_ref[...])))
    time_query = packed_ref[:, :WIDTH]

    def of_round(index, column):
        value = packed_ref[index * 64 : index * 64 + 64, column : column + WIDTH]
        return jnp.concatenate([value] * ROUNDS, axis=0)

    temporal = Attention(
        gather_ref,
        spread_ref,
        (0, 1, 2, 3),
        lambda index: of_round(index, WIDTH),
        lambda index: of_round(index, 2 * WIDTH),
        lax.div(lanes, 16) <= lax.div(iota((TOKENS, 128), 0), 64),
    )
    mixed_two = low(temporal.forward(time_query))
    after_time = after_tanner + dot(mixed_two, w_temporal_out_ref[...])

    def put(target, slab, value):
        for half in range(value.shape[1] // 128):
            target[(slab + half) * 256 : (slab + half + 1) * 256] = low(value[:, half * 128 : half * 128 + 128])

    unit_three, inverse_three, hidden_three = norm(after_time, gain_ffn_ref[...])
    cotangent = cotangent_ref[...]
    for block in range(FF // WIDTH):
        part = slice(block * WIDTH, (block + 1) * WIDTH)
        before = dot(hidden_three, w_up_ref[:, part])
        square = before * before
        bend = jnp.tanh(GELU * before * (1.0 + 0.044715 * square))
        activated_ref[:, part] = low(0.5 * before * (1.0 + bend))
        slope = 0.5 * (1.0 + bend) + 0.5 * before * (1.0 - bend * bend) * (GELU * (1.0 + 3 * 0.044715 * square))
        before_ref[:, part] = low(dot_back(cotangent, w_down_ref[part]) * slope)
    for block in range(FF // WIDTH):
        part = slice(block * WIDTH, (block + 1) * WIDTH)
        put(early_ref, 2 * block, dot_weight(activated_ref[:, part], cotangent))
    put(early_ref, 8, dot_weight(hidden_three, before_ref[...]))
    early.core_out()
    grad_three = dot_back(before_ref[...], w_up_ref[...])
    grad_norm, grad_gain_ffn = norm_back(grad_three, unit_three, inverse_three, gain_ffn_ref[...])
    grad_after_time = wide(cotangent) + grad_norm

    grad_low = low(grad_after_time)
    put(middle_ref, 6, dot_weight(mixed_two, grad_low))
    grad_mixed = dot_back(grad_low, w_temporal_out_ref[...])

    def over_rounds(value):
        return (value[:64] + value[64:128]) + (value[128:192] + value[192:])

    def put_time(index, grad_key, grad_value):
        grad_packed_ref[index * 64 : index * 64 + 64, WIDTH : 2 * WIDTH] = low(over_rounds(grad_key))
        grad_packed_ref[index * 64 : index * 64 + 64, 2 * WIDTH :] = low(over_rounds(grad_value))

    grad_packed_ref[:, :WIDTH] = low(temporal.backward(time_query, grad_mixed, put_time))
    early.core_in()
    put(middle_ref, 0, dot_weight(hidden_two, grad_packed_ref[...]))
    middle.core_out()
    grad_two = dot_back(grad_packed_ref[...], w_temporal_ref[...])
    grad_norm, grad_gain_time = norm_back(grad_two, unit_two, inverse_two, gain_time_ref[...])
    grad_after_tanner = grad_after_time + grad_norm

    grad_low = low(grad_after_tanner)
    put(late_ref, 6, dot_weight(mixed_one, grad_low))
    grad_mixed = dot_back(grad_low, w_merge_ref[...])

    def put_tanner(index, grad_key, grad_value):
        for grad, part in ((grad_key, slice(0, WIDTH)), (grad_value, slice(WIDTH, 2 * WIDTH))):
            if index == 0:
                own_grad_ref[:, part] = grad
            elif index == 1:
                rows_grad_ref[:, part] = grad
            elif index == 4:
                columns_grad_ref[:, part] = grad
            elif index in (2, 3):
                by = offsets_ref[1, index - 1]
                turned = turn(grad, by)
                own_grad_ref[:, part] += jnp.where(column >= by, turned, 0.0)
                columns_grad_ref[:, part] += jnp.where(column >= by, 0.0, turned)
            else:
                padded_ref[index - 5, :, 8:16, :, part] = grad.reshape(ROUNDS, 8, 8, WIDTH)

    query_low = low(tanner.backward(query, grad_mixed, put_tanner))
    middle.core_in()
    own_grad, rows_grad = own_grad_ref[...], rows_grad_ref[...]
    for index in (5, 6):
        by = offsets_ref[0, index - 1]
        own_grad = own_grad + padded_ref[index - 5, :, pl.ds(8 - by, 8)].reshape(TOKENS, 2 * WIDTH)
        rows_grad = rows_grad + padded_ref[index - 5, :, pl.ds(16 - by, 8)].reshape(TOKENS, 2 * WIDTH)
    rows_low, own_low, columns_low = low(rows_grad), low(own_grad), low(columns_grad_ref[...])
    put(late_ref, 0, dot_weight(hidden_one, query_low))
    put(
        late_ref,
        2,
        dot_weight(hidden_one, own_low)
        + dot_weight(hidden_ref[TOKENS : 2 * TOKENS], rows_low)
        + dot_weight(hidden_ref[2 * TOKENS :], columns_low),
    )
    late.core_out()
    back_out_ref[1] = low(dot_back(columns_low, w_key_value_ref[...]))
    back_columns = send(3, back_out_ref.at[1], back_in_ref.at[1], place.column_tile(1))
    back_out_ref[0] = low(dot_back(rows_low, w_key_value_ref[...]))
    back_rows = send(2, back_out_ref.at[0], back_in_ref.at[0], place.row_tile(1))
    grad_one = dot_back(query_low, w_query_ref[...]) + dot_back(own_low, w_key_value_ref[...])
    late.core_in()
    early.strip_in()
    middle.strip_in()
    back_rows.wait()
    back_columns.wait()
    grad_one = grad_one + (wide(back_in_ref[0]) + wide(back_in_ref[1]))
    grad_norm, grad_gain_tanner = norm_back(grad_one, unit_one, inverse_one, gain_tanner_ref[...])
    grad_embedded = grad_after_tanner + grad_norm
    upper, lower = halves(grad_embedded)
    from_table = dot_weight(features, upper) + dot_weight(features, lower)
    row = iota((SMALL_ROWS, WIDTH), 0)
    shares = jnp.where(row == 9, grad_gain_tanner, from_table)
    shares = jnp.where(row == 10, grad_gain_time, shares)
    shares = jnp.where(row == 11, grad_gain_ffn, shares)
    small.out(0, shares)
    token_grad_ref[...] = upper
    early.plane_in()
    middle.plane_in()
    late.strip_in()
    small.out(1, small.total())
    late.plane_in()
    early.z_in()
    middle.z_in()
    small.out(2, small.total())
    late.z_in()
    early.strip_gathered()
    middle.strip_gathered()
    late.strip_gathered()
    early.plane_gathered()
    middle.plane_gathered()
    late.plane_gathered()
    small_result_ref[...] = small.total()
    early.finish()
    middle.finish()
    late.finish()


def window(*operands):
    vmem = pl.BlockSpec(memory_space=pltpu.VMEM)
    specs = [vmem] * len(operands)
    for index in (7, 8, 9, 11, 12, 14, 15, 16):
        specs[index] = pl.BlockSpec(memory_space=pltpu.HBM)
    bf16, f32 = jnp.bfloat16, jnp.float32
    return pl.pallas_call(
        window_kernel,
        name="window",
        out_shape=(
            jax.ShapeDtypeStruct((RESULT_ROWS, 128), bf16),
            jax.ShapeDtypeStruct((SMALL_ROWS, WIDTH), f32),
            jax.ShapeDtypeStruct((TOKENS, WIDTH), bf16),
        ),
        in_specs=specs,
        out_specs=(vmem, vmem, vmem),
        scratch_shapes=[
            *[pltpu.VMEM(operands[index].shape, bf16) for index in (7, 8, 9, 11, 12, 14, 15, 16)],
            pltpu.SemaphoreType.DMA((8,)),
            pltpu.VMEM((4 * HALF, 128), bf16),
            pltpu.VMEM((2 * HALF, 128), bf16),
            pltpu.VMEM((2 * HALF, 128), bf16),
            pltpu.VMEM((NEIGHBOURS * WIDTH, 128), bf16),
            pltpu.VMEM((256, NEIGHBOURS * WIDTH), bf16),
            pltpu.VMEM((3 * TOKENS, WIDTH), bf16),
            pltpu.VMEM((2, TOKENS, WIDTH), bf16),
            pltpu.VMEM((2, TOKENS, WIDTH), bf16),
            pltpu.VMEM((ROUNDS, 16, 8, 2 * WIDTH), f32),
            pltpu.VMEM((NEIGHBOURS, TOKENS, 2 * WIDTH), f32),
            pltpu.VMEM((2, ROUNDS, 24, 8, 2 * WIDTH), f32),
            pltpu.VMEM((TOKENS, 2 * WIDTH), f32),
            pltpu.VMEM((TOKENS, 2 * WIDTH), f32),
            pltpu.VMEM((TOKENS, 2 * WIDTH), f32),
            pltpu.VMEM((TOKENS, FF), bf16),
            pltpu.VMEM((TOKENS, FF), bf16),
            pltpu.VMEM((TOKENS, 3 * WIDTH), f32),
            pltpu.VMEM((TOKENS, 3 * WIDTH), bf16),
            pltpu.SemaphoreType.DMA((4,)),
            pltpu.SemaphoreType.DMA((4,)),
            *SmallSum.SCRATCH,
            *TwoStepSum.scratch(2 * HALF),
            *TwoStepSum.scratch(HALF),
            *TwoStepSum.scratch(HALF),
        ],
        compiler_params=pltpu.CompilerParams(
            collective_id=0, has_side_effects=True, vmem_limit_bytes=36 * 2**20),
    )(*[pltpu.with_memory_space_constraint(x, pltpu.HBM) for x in operands])


def finish_kernel(scale, slabs_ref, small_ref, token_grad_in_ref, *outs):
    (token_grad_ref, flip_ref, plan_ref, gain_tanner_ref, query_ref, key_value_ref, merge_ref,
     gain_time_ref, temporal_ref, temporal_out_ref, gain_ffn_ref, up_ref, down_ref) = outs
    token_grad_ref[...] = token_grad_in_ref[...]
    small = small_ref[...] * scale
    plan_ref[...] = small[:8]
    flip_ref[...] = small[8:9]
    gain_tanner_ref[...] = small[9:10]
    gain_time_ref[...] = small[10:11]
    gain_ffn_ref[...] = small[11:12]

    def take(target, slab):
        for block in range(target.shape[0] // 256):
            for half in range(target.shape[1] // 128):
                target[block * 256 : block * 256 + 256, half * 128 : half * 128 + 128] = (
                    wide(slabs_ref[slab * 256 : slab * 256 + 256]) * scale)
                slab += 1

    take(down_ref, 0)
    take(up_ref, 8)
    take(temporal_ref, 16)
    take(temporal_out_ref, 22)
    take(query_ref, 24)
    take(key_value_ref, 26)
    take(merge_ref, 30)


def finish(scale, slabs, small, token_grad):
    vmem = pl.BlockSpec(memory_space=pltpu.VMEM)
    f32 = jnp.float32
    return pl.pallas_call(
        lambda *refs: finish_kernel(scale, *refs),
        name="finish",
        out_shape=(
            jax.ShapeDtypeStruct((TOKENS, WIDTH), jnp.bfloat16),
            jax.ShapeDtypeStruct((1, WIDTH), f32),
            jax.ShapeDtypeStruct((PLAN_STEP_COUNT, WIDTH), f32),
            jax.ShapeDtypeStruct((1, WIDTH), f32),
            jax.ShapeDtypeStruct((WIDTH, WIDTH), f32),
            jax.ShapeDtypeStruct((WIDTH, 2 * WIDTH), f32),
            jax.ShapeDtypeStruct((WIDTH, WIDTH), f32),
            jax.ShapeDtypeStruct((1, WIDTH), f32),
            jax.ShapeDtypeStruct((WIDTH, 3 * WIDTH), f32),
            jax.ShapeDtypeStruct((WIDTH, WIDTH), f32),
            jax.ShapeDtypeStruct((1, WIDTH), f32),
            jax.ShapeDtypeStruct((WIDTH, FF), f32),
            jax.ShapeDtypeStruct((FF, WIDTH), f32),
        ),
        in_specs=[vmem] * 3,
        out_specs=(vmem,) * 13,
        compiler_params=pltpu.CompilerParams(vmem_limit_bytes=32 * 2**20),
    )(slabs, small, token_grad)


def on_device(
    tokens,
    syndrome,
    check_plan_step,
    offsets,
    flip_vector,
    plan_step_embedding,
    gain_tanner,
    w_query,
    w_key_value,
    w_merge,
    gain_time,
    w_temporal,
    w_temporal_out,
    gain_ffn,
    w_ffn_up,
    w_ffn_down,
    cotangent,
):
    tile = tokens.shape
    devices = lax.axis_size("gx") * lax.axis_size("gy")
    scale = 1.0 / math.sqrt(tile[0] * tile[1] * tile[2] * devices)
    slabs, small, token_grad = window(
        tokens.reshape(TOKENS, WIDTH),
        syndrome.reshape(TOKENS // 8, 8),
        check_plan_step.reshape(TOKENS // 8, 8),
        offsets.T,
        flip_vector.reshape(1, WIDTH),
        plan_step_embedding,
        gain_tanner.reshape(1, WIDTH),
        w_query,
        w_key_value,
        w_merge,
        gain_time.reshape(1, WIDTH),
        w_temporal,
        w_temporal_out,
        gain_ffn.reshape(1, WIDTH),
        w_ffn_up,
        w_ffn_down,
        cotangent.reshape(TOKENS, WIDTH),
    )
    outs = list(finish(scale, slabs, small, token_grad))
    outs[0] = outs[0].reshape(tile)
    for index in (1, 3, 7, 10):
        outs[index] = outs[index].reshape(WIDTH)
    return tuple(outs)


def solution(mesh):
    return jax.shard_map(
        on_device,
        mesh=mesh,
        in_specs=(
            P(None, "gx", "gy", None),
            P(None, "gx", "gy"),
            P(None, "gx", "gy"),
            P(),
            P(),
            P(),
            P(),
            P(),
            P(),
            P(),
            P(),
            P(),
            P(),
            P(),
            P(),
            P(),
            P(None, "gx", "gy", None),
        ),
        out_specs=(
            P(None, "gx", "gy", None),
            P(),
            P(),
            P(),
            P(),
            P(),
            P(),
            P(),
            P(),
            P(),
            P(),
            P(),
            P(),
        ),
        check_vma=False,
    )
```

profile of v0, /device:TPU:1, one launch (start us, length us, event | category | flops | bytes accessed | tf_op | source)
XLA Modules:
  0.0 62.9 jit_solution(480947839026749767)
XLA Ops:
  0.7 59.9 %window.1 = (bf16[8192,128]{1,0:T(8,128)(2,1)S(1)}, f32[16,256]{1,0:T(8,128)S(1)}, bf16[256,256]{1,0:T(8,128)(2,1)S(1)}) custom-call(bf16[256,256]{1,0:T(8,128)(2,1)} %bitcast.14, s32[32,8]{1,0:T(8,128)} %bitcast.16, s32[32,8]{1,0:T(8,128)} %bitcast.17, s32[2,6]{1,0:T(2,128)} %bitcast.18, f32[1,256]{1,0:T(1,128)} %bitcast.19, f32[8,256]{1,0:T(8,128)} %embedding_ref.1, ...), custom_call_target="tpu_custom_call" | custom-call | tf_op jit(solution)/shard_map/window/pallas_call | solution.py:748
  60.5 2.4 %finish.1 = (bf16[256,256]{1,0:T(8,128)(2,1)}, f32[1,256]{1,0:T(1,128)}, f32[8,256]{1,0:T(8,128)}, f32[1,256]{1,0:T(1,128)}, f32[256,256]{1,0:T(8,128)}, /*index...) custom-call(bf16[8192,128]{1,0:T(8,128)(2,1)S(1)} %get-tuple-element, ...), custom_call_target="tpu_custom_call" | custom-call | tf_op jit(solution)/shard_map/finish/pallas_call | solution.py:821
where the time goes:
time: 63 us; the launch traced here: 62.9 us
  Pallas kernels  62.2 us (99%)
  between operations  0.66 us (1%)
    pallas_call x1, Pallas kernels, window(): pl.pallas_call(window_kernel, name='window', out_shape=(jax.ShapeDtypeStr...  59.9 us
    pallas_call x1, Pallas kernels, finish(): pl.pallas_call(lambda *refs: finish_kernel(scale, *refs), name='finish',...  2.35 us

commit v1 on v0

--- a/solution.py
+++ b/solution.py
@@ -261,10 +261,7 @@
         p = self.place
         for copy in self.copies:
             copy.wait()
-        total = self.along_z[0].astype(jnp.float32)
-        for index in range(1, 8):
-            total = total + self.along_z[index].astype(jnp.float32)
-        total = total.astype(jnp.bfloat16)
+        total = self.z_total()
         first = rows(self.base + p.x * self.strip + p.y * self.chunk, self.chunk)
         second = rows(self.base + self.half // 2 + p.y * self.strip + p.x * self.chunk, self.chunk)
         self.result[first] = total[: self.chunk]
@@ -294,30 +291,89 @@
             strip = self.strip_of(part, lax.rem((p.x, p.y)[part] + 4 - step, 4))
             self.core_copies.append(self.copy(34 + index, strip, strip, p.other_core()))
 
+    def z_total(self):
+        total = self.along_z[0].astype(jnp.float32)
+        for index in range(1, 8):
+            total = total + self.along_z[index].astype(jnp.float32)
+        return total.astype(jnp.bfloat16)
+
+
+class ThreeStepSum(TwoStepSum):
+    @staticmethod
+    def scratch(half):
+        bf16 = jnp.bfloat16
+        return (
+            *TwoStepSum.scratch(half)[:5],
+            pltpu.VMEM((2, half // 16, 128), bf16),
+            pltpu.SemaphoreType.DMA((47,)),
+            pltpu.SemaphoreType.DMA((47,)),
+            pltpu.VMEM((7, half // 128, 128), bf16),
+        )
+
+    def __init__(self, place, half, base, source, result, scratch):
+        super().__init__(place, half, base, source, result, scratch[:8])
+        self.in_z = scratch[8]
+        self.part = half // 128
+
+    def plane_in(self):
+        p = self.place
+        for copy in self.copies:
+            copy.wait()
+        for part, own in ((0, p.y * self.chunk), (1, p.x * self.chunk)):
+            total = self.two[part, rows(own, self.chunk)].astype(jnp.float32)
+            for index in range(3):
+                total = total + self.in_two[part * 3 + index].astype(jnp.float32)
+            self.along_z[0, part * self.chunk : (part + 1) * self.chunk] = total.astype(jnp.bfloat16)
+        self.copies = []
+        for index, step in enumerate(Z_STEPS):
+            z = lax.rem(p.z + step, 8)
+            share = self.along_z.at[0, rows(z * self.part, self.part)]
+            self.copies.append(self.copy(13 + index, share, self.in_z.at[index], p.at_z(z)))
+
+    def part_in(self):
+        p = self.place
+        for copy in self.copies:
+            copy.wait()
+        own = rows(p.z * self.part, self.part)
+        total = self.along_z[0, own].astype(jnp.float32)
+        for index in range(7):
+            total = total + self.in_z[index].astype(jnp.float32)
+        self.along_z[1, own] = total.astype(jnp.bfloat16)
+        share = self.along_z.at[1, own]
+        self.copies = []
+        for index, step in enumerate(Z_STEPS):
+            self.copies.append(self.copy(40 + index, share, share, p.at_z(lax.rem(p.z + step, 8))))
+
+    def z_total(self):
+        return self.along_z[1]
+
 
 class SmallSum:
     SCRATCH = (
         pltpu.VMEM((2, SMALL_ROWS, 256), jnp.bfloat16),
-        pltpu.VMEM((16, SMALL_ROWS, 256), jnp.bfloat16),
+        pltpu.VMEM((4, SMALL_ROWS, 256), jnp.bfloat16),
+        pltpu.VMEM((4, SMALL_ROWS, 256), jnp.bfloat16),
         pltpu.VMEM((8, SMALL_ROWS, 256), jnp.bfloat16),
-        pltpu.SemaphoreType.DMA((23,)),
-        pltpu.SemaphoreType.DMA((23,)),
+        pltpu.SemaphoreType.DMA((14,)),
+        pltpu.SemaphoreType.DMA((14,)),
     )
 
     def __init__(self, place, scratch):
         self.place = place
-        self.slots = scratch[:3]
-        self.send, self.recv = scratch[3:]
+        self.slots = scratch[:4]
+        self.send, self.recv = scratch[4:]
 
     def out(self, stage, value):
         p = self.place
         self.stage = stage
         slots = self.slots[stage]
-        mine = (p.core, p.x * 4 + p.y, p.z)[stage]
+        mine = (p.core, p.x, p.y, p.z)[stage]
         if stage == 0:
             peers = [p.other_core()]
         elif stage == 1:
-            peers = [p.in_plane(lax.rem(p.x + x, 4), lax.rem(p.y + y, 4)) for x, y in PLANE_STEPS]
+            peers = [p.at_x(lax.rem(p.x + step, 4)) for step in (2, 1, 3)]
+        elif stage == 2:
+            peers = [p.at_y(lax.rem(p.y + step, 4)) for step in (2, 1, 3)]
         else:
             peers = [p.at_z(lax.rem(p.z + step, 8)) for step in Z_STEPS]
         slots[mine] = value.astype(jnp.bfloat16)
@@ -326,8 +382,8 @@
             copy = pltpu.make_async_remote_copy(
                 src_ref=slots.at[mine],
                 dst_ref=slots.at[mine],
-                send_sem=self.send.at[(0, 1, 16)[stage] + index],
-                recv_sem=self.recv.at[(0, 1, 16)[stage] + index],
+                send_sem=self.send.at[(0, 1, 4, 7)[stage] + index],
+                recv_sem=self.recv.at[(0, 1, 4, 7)[stage] + index],
                 device_id=peer,
                 device_id_type=MESH,
             )
@@ -511,7 +567,7 @@
         load = pltpu.make_async_copy(source, target, loaded.at[index])
         load.start()
         loads.append(load)
-    groups = ((TwoStepSum, 2 * HALF, 0, early_ref), (TwoStepSum, HALF, 4 * HALF, middle_ref), (TwoStepSum, HALF, 6 * HALF, late_ref))
+    groups = ((ThreeStepSum, 2 * HALF, 0, early_ref), (TwoStepSum, HALF, 4 * HALF, middle_ref), (TwoStepSum, HALF, 6 * HALF, late_ref))
     ends = [len(SmallSum.SCRATCH)]
     for kind, half, _, _ in groups:
         ends.append(ends[-1] + len(kind.scratch(half)))
@@ -705,6 +761,8 @@
     late.core_in()
     early.strip_in()
     middle.strip_in()
+    late.strip_in()
+    early.plane_in()
     back_rows.wait()
     back_columns.wait()
     grad_one = grad_one + (wide(back_in_ref[0]) + wide(back_in_ref[1]))
@@ -718,20 +776,20 @@
     shares = jnp.where(row == 11, grad_gain_ffn, shares)
     small.out(0, shares)
     token_grad_ref[...] = upper
-    early.plane_in()
     middle.plane_in()
-    late.strip_in()
     small.out(1, small.total())
     late.plane_in()
+    early.part_in()
+    small.out(2, small.total())
+    middle.z_in()
+    late.z_in()
     early.z_in()
-    middle.z_in()
-    small.out(2, small.total())
-    late.z_in()
+    small.out(3, small.total())
+    middle.strip_gathered()
     early.strip_gathered()
-    middle.strip_gathered()
     late.strip_gathered()
+    middle.plane_gathered()
     early.plane_gathered()
-    middle.plane_gathered()
     late.plane_gathered()
     small_result_ref[...] = small.total()
     early.finish()
@@ -779,7 +837,7 @@
             pltpu.SemaphoreType.DMA((4,)),
             pltpu.SemaphoreType.DMA((4,)),
             *SmallSum.SCRATCH,
-            *TwoStepSum.scratch(2 * HALF),
+            *ThreeStepSum.scratch(2 * HALF),
             *TwoStepSum.scratch(HALF),
             *TwoStepSum.scratch(HALF),
         ],

time: 63 us -> 60.9 us (0.967)
  Pallas kernels: 62.2 us -> 60.1 us
    pallas_call x1, Pallas kernels: 59.9 us -> 57.8 us  [window(): pl.pallas_call(window_kernel, name='window', out_shape=(jax.ShapeDtypeStr...]
where the time goes in v1:
time: 60.9 us; the launch traced here: 60.8 us
  Pallas kernels  60.1 us (99%)
  between operations  0.66 us (1%)
    pallas_call x1, Pallas kernels, window(): pl.pallas_call(window_kernel, name='window', out_shape=(jax.ShapeDtypeStr...  57.8 us
    pallas_call x1, Pallas kernels, finish(): pl.pallas_call(lambda *refs: finish_kernel(scale, *refs), name='finish',...  2.35 us

profile of v1, /device:TPU:1, one launch (start us, length us, event | category | flops | bytes accessed | tf_op | source)
XLA Modules:
  0.0 60.8 jit_solution(14623871146388111164)
XLA Ops:
  0.7 57.8 %window.1 = (bf16[8192,128]{1,0:T(8,128)(2,1)S(1)}, f32[16,256]{1,0:T(8,128)S(1)}, bf16[256,256]{1,0:T(8,128)(2,1)S(1)}) custom-call(bf16[256,256]{1,0:T(8,128)(2,1)} %bitcast.14, s32[32,8]{1,0:T(8,128)} %bitcast.16, s32[32,8]{1,0:T(8,128)} %bitcast.17, s32[2,6]{1,0:T(2,128)} %bitcast.18, f32[1,256]{1,0:T(1,128)} %bitcast.19, f32[8,256]{1,0:T(8,128)} %embedding_ref.1, ...), custom_call_target="tpu_custom_call" | custom-call | tf_op jit(solution)/shard_map/window/pallas_call | solution.py:806
  58.4 2.4 %finish.1 = (bf16[256,256]{1,0:T(8,128)(2,1)}, f32[1,256]{1,0:T(1,128)}, f32[8,256]{1,0:T(8,128)}, f32[1,256]{1,0:T(1,128)}, f32[256,256]{1,0:T(8,128)}, /*index...) custom-call(bf16[8192,128]{1,0:T(8,128)(2,1)S(1)} %get-tuple-element, ...), custom_call_target="tpu_custom_call" | custom-call | tf_op jit(solution)/shard_map/finish/pallas_call | solution.py:879
